TPU v7x, 32 devices: a whole 2x2x4 slice. The times are simulated.
32 devices in a mesh: blk: 4 (over y, core), layer: 4 (over z), shard: 2 (over x).
Axes of the slice: x: 2, y: 2, z: 4, core: 2. Of those that a mesh axis runs over, the one named last changes fastest.
Arguments:
- train_grads: bfloat16 [8192, 4, 4096], P(('blk', 'shard'), 'layer'), may hold values from -6 to 6
- query_grads: bfloat16 [256, 4, 4096], P(('blk', 'shard'), 'layer'), may hold values from -6 to 6
- in_factor: bfloat16 [4, 64, 64], P('layer'), as said below
- out_factor: bfloat16 [4, 64, 64], P('layer'), as said below
Outputs:
- scores: float32 [256, 8192], P('layer', ('blk', 'shard'))
Inputs may be any that keep to these rules, and one draw needn't show every extreme that they name: `in_factor`: Symmetric, with a dominant positive diagonal. `out_factor`: Symmetric, with a dominant positive diagonal.
All inputs are finite; a program needn't handle non-finite values.
Results may differ from a plain program's by a relative error of at most 0.012.
Values may be sent and summed in bfloat16 or wider, within the bound.
A program may use at most 64 MiB of HBM per device.

v0:
```python
import jax
import jax.numpy as jnp
from jax import lax
from jax.sharding import PartitionSpec as P

score_scale = 1.0 / 128.0


def precondition(rows, inward, outward):
    count = rows.shape[0]
    proj = inward.shape[0]
    cube = rows.reshape(count, proj, proj)
    half = jnp.einsum("nio,op->nip", cube, outward, preferred_element_type=jnp.float32).astype(
        jnp.bfloat16
    )
    ready = jnp.einsum("ji,nip->njp", inward, half, preferred_element_type=jnp.float32).astype(
        jnp.bfloat16
    )
    return ready.reshape(count, proj * proj)


def per_device(train_grads, query_grads, in_factor, out_factor):
    train_rows = train_grads[:, 0, :]
    panel = query_grads[:, 0, :]
    inward = in_factor[0]
    outward = out_factor[0]
    own_ready = precondition(panel, inward, outward)
    gathered = lax.all_gather(own_ready, ("blk", "shard"), axis=0, tiled=True)
    return lax.psum_scatter(
        (
            jnp.einsum("qk,nk->qn", gathered, train_rows, preferred_element_type=jnp.float32)
            * score_scale
        ).astype(jnp.bfloat16),
        "layer",
        scatter_dimension=0,
        tiled=True,
    ).astype(jnp.float32)


def solution(mesh):
    in_specs = (
        P(("blk", "shard"), "layer", None),
        P(("blk", "shard"), "layer", None),
        P("layer", None, None),
        P("layer", None, None),
    )
    out_specs = P("layer", ("blk", "shard"))
    return jax.shard_map(
        per_device, mesh=mesh, in_specs=in_specs, out_specs=out_specs, check_vma=False
    )
```

profile of v0, /device:TPU:0, one launch (start us, length us, event | category | flops | bytes accessed | tf_op | source)
XLA Modules:
  0.0 79.3 jit_solution(15213127202555348229)
XLA Ops:
  6.5 0.0 copy-start
  6.5 0.0 all-gather.2.cloned.1.call-start
  6.5 1.5 %reshape_squeeze.3 = bf16[32,64,64]{2,1,0:T(8,128)(2,1)S(1)} reshape(bf16[32,1,4096]{2,0,1:T(8,128)(2,1)} %param.5) | data formatting | bytes 524288 | tf_op jit(solution)/shard_map/reshape;squeeze | solution.py:12
  8.0 0.0 copy-done
  8.0 1.5 %fusion.8 = bf16[32,64,64]{1,2,0:T(8,128)(2,1)S(1)} fusion(bf16[32,64,64]{2,1,0:T(8,128)(2,1)S(1)} %reshape_squeeze.3, bf16[1,64,64]{2,1,0:T(8,128)(2,1)S(1)} %copy-done, bf16[1,64,64]{2,1,0:T(8,128)(2,1)} %param.7), kind=kOutput, calls=%fused_computation.6 | convolution fusion | flops 33816576 | bytes 540672 | tf_op jit(solution)/shard_map/ji,nip->njp/dot_general | solution.py:16
  9.5 0.3 copy.5
  9.8 1.2 %reshape.3 = bf16[32,4096]{1,0:T(8,128)(2,1)} reshape(bf16[32,64,64]{2,1,0:T(8,128)(2,1)S(1)} %copy.5) | data formatting | bytes 524288 | tf_op jit(solution)/shard_map/reshape | solution.py:19
  11.0 0.0 all-gather.2.cloned.1.call-update
  11.0 0.0 reduce-scatter.2.cloned.1.call-start
  11.1 30.6 %all-gather.2.cloned.1.call-done = bf16[256,4096]{1,0:T(8,128)(2,1)} async-done(((bf16[32,4096]{1,0:T(8,128)(2,1)}), bf16[256,4096]{1,0:T(8,128)(2,1)}) %all-gather.2.cloned.1.call-update) | async-done | bytes 2097168 | tf_op jit(solution)/shard_map/all_gather | solution.py:28
  41.7 7.2 %fusion.5 = bf16[256,1024]{1,0:T(8,128)(2,1)} fusion(bf16[256,4096]{1,0:T(8,128)(2,1)} %all-gather.2.cloned.1.call-done, bf16[1024,1,4096]{2,0,1:T(8,128)(2,1)} %param.4), kind=kOutput, calls=%fused_computation.3 | convolution fusion | flops 2148007936 | bytes 11010048 | tf_op jit(solution)/shard_map/qk,nk->qn/dot_general | solution.py:31
  48.9 0.0 reduce-scatter.2.cloned.1.call-update
  48.9 22.0 %reduce-scatter.2.cloned.1.call-done = bf16[64,1024]{1,0:T(8,128)(2,1)} async-done(((bf16[256,1024]{1,0:T(8,128)(2,1)}), bf16[64,1024]{1,0:T(8,128)(2,1)}) %reduce-scatter.2.cloned.1.call-update) | async-done | bytes 131088 | tf_op jit(solution)/shard_map/reduce_scatter | solution.py:29
  70.9 1.6 %convert_element_type.19 = f32[64,1024]{1,0:T(8,128)} convert(bf16[64,1024]{1,0:T(8,128)(2,1)} %reduce-scatter.2.cloned.1.call-done) | non-fusion elementwise | flops 65536 | bytes 393216 | tf_op jit(solution)/shard_map/convert_element_type | solution.py:37
Async XLA Ops:
  6.5 1.5 %copy-start = (bf16[1,64,64]{2,1,0:T(8,128)(2,1)S(1)}, bf16[1,64,64]{2,1,0:T(8,128)(2,1)}, u32[]{:S(2)}) copy-start(bf16[1,64,64]{2,1,0:T(8,128)(2,1)} %param.6) | copy-start | bytes 24580
  6.5 35.1 %all-gather.2.cloned.1.call-start = ((), (), s32[]{:S(2)}) async-start(), calls=%async_computation.1 | async-start | bytes 2359296 | tf_op jit(solution)/shard_map/all_gather | solution.py:28
  11.0 59.9 %reduce-scatter.2.cloned.1.call-start = ((), (), s32[]{:S(2)}) async-start(), calls=%async_computation.2 | async-start | bytes 655360 | tf_op jit(solution)/shard_map/reduce_scatter | solution.py:29
Sparse Core Ops, SparseCore 0:
  11.1 30.4 all-gather.1
  49.0 21.8 reduce-scatter.1
where the time goes:
time: 79.6 us; the launch traced here: 79.3 us
  waiting for transfers between devices  52.6 us (66%)
  between operations  13.4 us (17%)
  matrix products  8.68 us (11%)
  local copies, waits for them, and re-layouts  2.93 us (4%)
  other arithmetic  1.62 us (2%)
    all_gather x1, waiting for transfers between devices, per_device(): gathered = lax.all_gather(own_ready, ('blk', 'shard'), axis=0, tiled=True)  30.6 us
    reduce_scatter x1, waiting for transfers between devices, per_device(): lax.psum_scatter((jnp.einsum('qk,nk->qn', gathered, train_rows, preferred...  22 us
    dot_general x1, matrix products, per_device(): jnp.einsum('qk,nk->qn', gathered, train_rows, preferred_element_type=jnp....  7.18 us
    convert_element_type x1, other arithmetic, per_device(): return lax.psum_scatter((jnp.einsum('qk,nk->qn', gathered, train_rows, pr...  1.62 us
  transfers between devices with their start and end apart: 2, of which 2 were waited for; matrix products, arithmetic and copies ran while one was open for 0% of the time, Pallas kernels for 0%

commit v1 on v0

v1 whole, which is shorter than its diff:
```python
import functools

import jax
import jax.numpy as jnp
from jax import lax
from jax.experimental import pallas as pl
from jax.experimental.pallas import tpu as pltpu
from jax.sharding import PartitionSpec as P

MESH = pl.DeviceIdType.MESH
score_scale = 1.0 / 128.0
bf16 = jnp.bfloat16
f32 = jnp.float32


def dot(a, b):
    return jnp.dot(a, b, preferred_element_type=f32)


def where_eq(shape, row_of, col_of):
    rows = lax.broadcasted_iota(jnp.int32, shape, 0)
    cols = lax.broadcasted_iota(jnp.int32, shape, 1)
    return (row_of(rows) == col_of(cols)).astype(f32).astype(bf16)


def precondition(query, inward, outward, spread, packed, own):
    rows, grad = query.shape
    proj = inward.shape[0]
    pair = proj // 2
    lanes = 2 * proj
    same = lambda v: v
    low = where_eq((proj, lanes), same, same)
    high = where_eq((proj, lanes), lambda r: r + proj, same)
    o_low = dot(outward, low)
    o_high = dot(outward, high)
    weight = jnp.concatenate(
        [jnp.concatenate([o_low, o_high], axis=1), jnp.concatenate([o_high, o_low], axis=1)], axis=0
    ).astype(bf16)
    stacked = jnp.concatenate([query[:, c * lanes : (c + 1) * lanes] for c in range(pair)], axis=0)
    half = dot(stacked, weight)
    for c in range(pair):
        part = half[c * rows : (c + 1) * rows]
        spread[pl.ds(c, rows, stride=proj), :] = part[:, :lanes]
        spread[pl.ds(pair + c, rows, stride=proj), :] = part[:, lanes:]
    split = where_eq((proj, proj), lambda r: 2 * (r % pair) + r // pair, same)
    ordered = dot(split, inward).astype(bf16)
    straight = where_eq((proj, proj), same, lambda k: 2 * (k % pair) + k // pair)
    crossed = where_eq((proj, proj), same, lambda k: 2 * (k % pair) + 1 - k // pair)
    row_id = lax.broadcasted_iota(jnp.int32, (proj, proj), 0)
    mixed = jnp.where(row_id < pair, dot(ordered, straight), dot(ordered, crossed)).astype(bf16)
    lane_id = lax.broadcasted_iota(jnp.int32, (pair, 2 * lanes), 1)
    for n in range(0, rows, 2):
        two = jnp.concatenate(
            [spread[pl.ds(n * proj, proj), :], spread[pl.ds((n + 1) * proj, proj), :]], axis=1
        ).astype(bf16)
        full = dot(mixed, two)
        ready = jnp.where(lane_id % lanes < proj, full[:pair], full[pair:])
        packed[pl.ds(n * pair, pair), :] = ready[:, :lanes]
        packed[pl.ds((n + 1) * pair, pair), :] = ready[:, lanes:]
    for d in range(pair):
        chunk = packed[pl.ds(d, rows, stride=pair), :].astype(bf16)
        own[0, :, d * lanes : (d + 1) * lanes] = chunk[: rows // 2]
        own[1, :, d * lanes : (d + 1) * lanes] = chunk[rows // 2 :]


def kernel(
    sizes,
    train_hbm,
    query_hbm,
    in_hbm,
    out_hbm,
    scores,
    train,
    query,
    inward,
    outward,
    spread,
    packed,
    pieces,
    terms,
    landed,
    load_sem,
    small_sem,
    send_sem,
    arrive,
    crossed,
    term_send,
    term_recv,
):
    n_blk, n_layer, n_shard = sizes
    n_core = 2 if n_blk % 2 == 0 else 1
    n_y = n_blk // n_core
    blk, layer, s = lax.axis_index("blk"), lax.axis_index("layer"), lax.axis_index("shard")
    y, c = blk // n_core, blk % n_core
    per_owner = n_blk * n_shard // n_layer
    tile = train.shape[1]

    y_at = lambda dy: lax.rem(y + dy, n_y)
    s_at = lambda ds: lax.rem(s + ds, n_shard)
    l_at = lambda dl: lax.rem(layer + dl, n_layer)
    blk_of = lambda yy, cc: yy * n_core + cc
    piece_of = lambda yy, cc, ss: blk_of(yy, cc) * n_shard + ss
    to_s = lambda ds: {"blk": blk, "layer": layer, "shard": s_at(ds)}
    to_y = lambda dy: {"blk": blk_of(y_at(dy), c), "layer": layer, "shard": s}
    to_core = {"blk": blk_of(y, 1 - c), "layer": layer, "shard": s}
    to_l = lambda ll: {"blk": blk, "layer": ll, "shard": s}

    barrier = pltpu.get_barrier_semaphore()
    friends = [to_s(ds) for ds in range(1, n_shard)] + [to_y(dy) for dy in range(1, n_y)]
    friends += [to_core] * (n_core - 1) + [to_l(l_at(dl)) for dl in range(1, n_layer)]
    for friend in friends:
        pl.semaphore_signal(barrier, inc=1, device_id=friend, device_id_type=MESH)

    smalls = [
        pltpu.make_async_copy(query_hbm, query, small_sem.at[0]),
        pltpu.make_async_copy(in_hbm, inward, small_sem.at[1]),
        pltpu.make_async_copy(out_hbm, outward, small_sem.at[2]),
    ]
    for copy in smalls:
        copy.start()
    loads = [
        pltpu.make_async_copy(train_hbm.at[pl.ds(t * tile, tile)], train.at[t], load_sem.at[t])
        for t in range(train.shape[0])
    ]
    for copy in loads:
        copy.start()
    for copy in smalls:
        copy.wait()

    mine = piece_of(y, c, s)
    precondition(query[...], inward[...], outward[...], spread, packed, pieces.at[mine])

    pl.semaphore_wait(barrier, len(friends))

    sent = []

    def send(index, h, sems, yy, ss, device):
        copy = pltpu.make_async_remote_copy(
            src_ref=pieces.at[index, h],
            dst_ref=pieces.at[index, h],
            send_sem=send_sem.at[len(sent)],
            recv_sem=sems.at[yy, ss, h],
            device_id=device,
            device_id_type=MESH,
        )
        copy.start()
        sent.append(copy)

    def wait(index, h, sems, yy, ss):
        pltpu.make_async_remote_copy(
            src_ref=pieces.at[index, h],
            dst_ref=pieces.at[index, h],
            send_sem=send_sem.at[0],
            recv_sem=sems.at[yy, ss, h],
            device_id=to_core,
            device_id_type=MESH,
        ).wait_recv()

    def pass_on(yy, ss, h):
        if n_core > 1:
            send(piece_of(yy, c, ss), h, crossed, yy, ss, to_core)

    def take(yy, ss, h):
        wait(piece_of(yy, c, ss), h, arrive, yy, ss)

    for h in range(2):
        pass_on(y, s, h)
    for h in range(2):
        for ds in range(1, n_shard):
            send(mine, h, arrive, y, s, to_s(ds))
        for dy in range(1, n_y):
            send(mine, 1 - h, arrive, y, s, to_y(dy))

    term_copies = []

    def term_copy(g):
        owner = g // per_owner
        return owner, pltpu.make_async_remote_copy(
            src_ref=terms.at[g],
            dst_ref=landed.at[layer, g % per_owner],
            send_sem=term_send.at[g],
            recv_sem=term_recv.at[layer, g % per_owner],
            device_id=to_l(owner),
            device_id_type=MESH,
        )

    def multiply(yy, ss):
        for other in range(1, n_core):
            for h in range(2):
                wait(piece_of(yy, 1 - c, ss), h, crossed, yy, ss)
        index = [piece_of(yy, cc, ss) for cc in range(n_core)]
        rows = query.shape[0]
        left = jnp.concatenate([pieces[g].reshape(rows, query.shape[1]) for g in index], axis=0)
        for t in range(train.shape[0]):
            if not term_copies:
                loads[t].wait()
            term = lax.dot_general(
                left, train[t], (((1,), (1,)), ((), ())), preferred_element_type=f32
            )
            term = (term * score_scale).astype(bf16)
            for k, g in enumerate(index):
                terms[g, :, t * tile : (t + 1) * tile] = term[k * rows : (k + 1) * rows]
        for g in index:
            owner, copy = term_copy(g)
            term_copies.append((owner, copy))

            @pl.when(owner != layer)
            def _():
                copy.start()

    multiply(y, s)
    for ds in range(1, n_shard):
        take(y, s_at(ds), 0)
        for dy in range(1, n_y):
            send(piece_of(y, c, s_at(ds)), 0, arrive, y, s_at(ds), to_y(dy))
        pass_on(y, s_at(ds), 0)
    for dy in range(1, n_y):
        take(y_at(dy), s, 1)
        for ds in range(1, n_shard):
            send(piece_of(y_at(dy), c, s), 1, arrive, y_at(dy), s, to_s(ds))
        pass_on(y_at(dy), s, 1)
    for ds in range(1, n_shard):
        take(y, s_at(ds), 1)
        pass_on(y, s_at(ds), 1)
    for dy in range(1, n_y):
        take(y_at(dy), s, 0)
        pass_on(y_at(dy), s, 0)
    for ds in range(1, n_shard):
        multiply(y, s_at(ds))
    for dy in range(1, n_y):
        for ds in range(1, n_shard):
            for h in range(2):
                take(y_at(dy), s_at(ds), h)
                pass_on(y_at(dy), s_at(ds), h)
    for dy in range(1, n_y):
        multiply(y_at(dy), s)
    for dy in range(1, n_y):
        for ds in range(1, n_shard):
            multiply(y_at(dy), s_at(ds))

    rows = query.shape[0]
    for j in range(per_owner):
        total = terms[layer * per_owner + j].astype(f32)
        for dl in range(1, n_layer):
            ll = l_at(dl)
            pltpu.make_async_remote_copy(
                src_ref=terms.at[0],
                dst_ref=landed.at[ll, j],
                send_sem=term_send.at[0],
                recv_sem=term_recv.at[ll, j],
                device_id=to_l(ll),
                device_id_type=MESH,
            ).wait_recv()
            total = total + landed[ll, j].astype(f32)
        scores[j * rows : (j + 1) * rows, :] = total

    for copy in sent:
        copy.wait_send()
    for owner, copy in term_copies:

        @pl.when(owner != layer)
        def _():
            copy.wait_send()


def solution(mesh):
    n_blk, n_layer, n_shard = mesh.shape["blk"], mesh.shape["layer"], mesh.shape["shard"]
    n_core = 2 if n_blk % 2 == 0 else 1
    n_y = n_blk // n_core

    def per_device(train_grads, query_grads, in_factor, out_factor):
        train_rows = train_grads[:, 0, :]
        panel = query_grads[:, 0, :]
        inward = in_factor[0]
        outward = out_factor[0]
        count, grad = train_rows.shape
        rows = panel.shape[0]
        proj = inward.shape[0]
        total = n_blk * n_shard
        per_owner = total // n_layer
        tiles = 4
        relay = 2 * (n_y - 1) * (n_shard - 1)
        sends = 2 * (n_y - 1 + n_shard - 1) + relay + 2 * n_y * n_shard * (n_core - 1)
        dma = pltpu.SemaphoreType.DMA
        return pl.pallas_call(
            functools.partial(kernel, (n_blk, n_layer, n_shard)),
            out_shape=jax.ShapeDtypeStruct((rows * per_owner, count), f32),
            in_specs=[pl.BlockSpec(memory_space=pl.ANY)] * 4,
            out_specs=pl.BlockSpec(memory_space=pltpu.VMEM),
            scratch_shapes=[
                pltpu.VMEM((tiles, count // tiles, grad), bf16),
                pltpu.VMEM((rows, grad), bf16),
                pltpu.VMEM((proj, proj), bf16),
                pltpu.VMEM((proj, proj), bf16),
                pltpu.VMEM((rows * proj, 2 * proj), f32),
                pltpu.VMEM((rows * proj // 2, 2 * proj), f32),
                pltpu.VMEM((total, 2, rows // 2, grad), bf16),
                pltpu.VMEM((total, rows, count), bf16),
                pltpu.VMEM((n_layer, per_owner, rows, count), bf16),
                dma((tiles,)),
                dma((3,)),
                dma((sends,)),
                dma((n_y, n_shard, 2)),
                dma((n_y, n_shard, 2)),
                dma((total,)),
                dma((n_layer, per_owner)),
            ],
            compiler_params=pltpu.CompilerParams(
                collective_id=0, has_side_effects=True, vmem_limit_bytes=56 * 1024 * 1024
            ),
        )(train_rows, panel, inward, outward)

    in_specs = (
        P(("blk", "shard"), "layer", None),
        P(("blk", "shard"), "layer", None),
        P("layer", None, None),
        P("layer", None, None),
    )
    out_specs = P("layer", ("blk", "shard"))
    return jax.shard_map(
        per_device, mesh=mesh, in_specs=in_specs, out_specs=out_specs, check_vma=False
    )
```

time: 79.6 us -> 35.8 us (0.45)
  the two profiles are of different devices: /device:TPU:0 before, /device:TPU:4 now
where the time goes in v1:
time: 35.8 us; the launch traced here: 35.7 us
  Pallas kernels  34 us (95%)
  local copies, waits for them, and re-layouts  1.67 us (5%)
    pallas_call x1, Pallas kernels, per_device(): pl.pallas_call(functools.partial(kernel, (n_blk, n_layer, n_shard)), out_...  34 us
    unnamed x1, local copies, waits for them, and re-layouts  1.67 us

profile of v1, /device:TPU:4, one launch (start us, length us, event | category | flops | bytes accessed | tf_op | source)
XLA Modules:
  0.0 35.7 jit_solution(17210733075042355229)
XLA Ops:
  0.0 34.0 %shard_map.46 = f32[64,1024]{1,0:T(8,128)} custom-call(bf16[1024,4096]{1,0:T(8,128)(2,1)} %bitcast.4, bf16[32,4096]{1,0:T(8,128)(2,1)} %bitcast.5, bf16[64,64]{1,0:T(8,128)(2,1)} %bitcast.6, bf16[64,64]{1,0:T(8,128)(2,1)} %bitcast.7), custom_call_target="tpu_custom_call" | custom-call | tf_op jit(solution)/shard_map/pallas_call | solution.py:285
  34.0 1.7 %copy.6 = f32[64,1024]{1,0:T(8,128)} copy(f32[64,1024]{1,0:T(8,128)} %shard_map.46) | data formatting | bytes 524288

commit v2 on v1

--- a/solution.py
+++ b/solution.py
@@ -79,6 +79,7 @@
     pieces,
     terms,
     landed,
+    gated,
     load_sem,
     small_sem,
     send_sem,
@@ -86,6 +87,7 @@
     crossed,
     term_send,
     term_recv,
+    gate_recv,
 ):
     n_blk, n_layer, n_shard = sizes
     n_core = 2 if n_blk % 2 == 0 else 1
@@ -171,44 +173,79 @@
         for dy in range(1, n_y):
             send(mine, 1 - h, arrive, y, s, to_y(dy))
 
-    term_copies = []
-
-    def term_copy(g):
-        owner = g // per_owner
-        return owner, pltpu.make_async_remote_copy(
+    half_l = n_layer // 2
+    side, place = layer // half_l, lax.rem(layer, half_l)
+    gate_of = lambda which: half_l - 1 + which
+    is_gate = layer == gate_of(side)
+    term_sent = []
+
+    def term_copy(g, dst, recv, ll):
+        return pltpu.make_async_remote_copy(
             src_ref=terms.at[g],
-            dst_ref=landed.at[layer, g % per_owner],
+            dst_ref=dst,
             send_sem=term_send.at[g],
-            recv_sem=term_recv.at[layer, g % per_owner],
-            device_id=to_l(owner),
+            recv_sem=recv,
+            device_id=to_l(ll),
             device_id_type=MESH,
         )
 
-    def multiply(yy, ss):
-        for other in range(1, n_core):
-            for h in range(2):
-                wait(piece_of(yy, 1 - c, ss), h, crossed, yy, ss)
-        index = [piece_of(yy, cc, ss) for cc in range(n_core)]
+    def owner_copy(g, slot):
+        j = lax.rem(g, per_owner)
+        return term_copy(g, landed.at[slot, j], term_recv.at[slot, j], g // per_owner)
+
+    def gate_copy(g, slot):
+        return term_copy(g, gated.at[slot, g], gate_recv.at[slot, g], gate_of(side))
+
+    loaded = []
+
+    def multiply(*chips):
+        for yy, ss in chips:
+            for other in range(1, n_core):
+                for h in range(2):
+                    wait(piece_of(yy, 1 - c, ss), h, crossed, yy, ss)
+        index = [piece_of(yy, cc, ss) for yy, ss in chips for cc in range(n_core)]
         rows = query.shape[0]
         left = jnp.concatenate([pieces[g].reshape(rows, query.shape[1]) for g in index], axis=0)
         for t in range(train.shape[0]):
-            if not term_copies:
+            if len(loaded) < train.shape[0]:
                 loads[t].wait()
+                loaded.append(t)
             term = lax.dot_general(
-                left, train[t], (((1,), (1,)), ((), ())), preferred_element_type=f32
+                train[t], left, (((1,), (1,)), ((), ())), preferred_element_type=f32
             )
-            term = (term * score_scale).astype(bf16)
+            term = (term * score_scale).T.astype(bf16)
             for k, g in enumerate(index):
                 terms[g, :, t * tile : (t + 1) * tile] = term[k * rows : (k + 1) * rows]
         for g in index:
-            owner, copy = term_copy(g)
-            term_copies.append((owner, copy))
-
-            @pl.when(owner != layer)
+            owner = g // per_owner
+            near = owner // half_l == side
+
+            @pl.when(jnp.logical_and(near, owner != layer))
             def _():
-                copy.start()
-
-    multiply(y, s)
+                owner_copy(g, place).start()
+
+            @pl.when(jnp.logical_and(jnp.logical_not(near), jnp.logical_not(is_gate)))
+            def _():
+                gate_copy(g, place).start()
+
+        term_sent.extend(index)
+        return index
+
+    def gather_gate(index):
+        for g in index:
+            far = g // per_owner // half_l != side
+
+            @pl.when(jnp.logical_and(far, is_gate))
+            def _():
+                total = terms[g].astype(f32)
+                for step in range(1, half_l):
+                    slot = lax.rem(place + step, half_l)
+                    gate_copy(g, slot).wait_recv()
+                    total = total + gated[slot, g].astype(f32)
+                terms[g] = total.astype(bf16)
+                owner_copy(g, half_l).start()
+
+    first = multiply((y, s))
     for ds in range(1, n_shard):
         take(y, s_at(ds), 0)
         for dy in range(1, n_y):
@@ -225,42 +262,35 @@
     for dy in range(1, n_y):
         take(y_at(dy), s, 0)
         pass_on(y_at(dy), s, 0)
-    for ds in range(1, n_shard):
-        multiply(y, s_at(ds))
-    for dy in range(1, n_y):
-        for ds in range(1, n_shard):
-            for h in range(2):
-                take(y_at(dy), s_at(ds), h)
-                pass_on(y_at(dy), s_at(ds), h)
-    for dy in range(1, n_y):
-        multiply(y_at(dy), s)
-    for dy in range(1, n_y):
-        for ds in range(1, n_shard):
-            multiply(y_at(dy), s_at(ds))
+    gather_gate(first)
+    beside = [(y, s_at(ds)) for ds in range(1, n_shard)] + [(y_at(dy), s) for dy in range(1, n_y)]
+    across = [(y_at(dy), s_at(ds)) for dy in range(1, n_y) for ds in range(1, n_shard)]
+    second = multiply(*beside) if beside else []
+    for yy, ss in across:
+        for h in range(2):
+            take(yy, ss, h)
+            pass_on(yy, ss, h)
+    third = multiply(*across) if across else []
+    gather_gate(second)
+    gather_gate(third)
 
     rows = query.shape[0]
     for j in range(per_owner):
-        total = terms[layer * per_owner + j].astype(f32)
-        for dl in range(1, n_layer):
-            ll = l_at(dl)
-            pltpu.make_async_remote_copy(
-                src_ref=terms.at[0],
-                dst_ref=landed.at[ll, j],
-                send_sem=term_send.at[0],
-                recv_sem=term_recv.at[ll, j],
-                device_id=to_l(ll),
-                device_id_type=MESH,
-            ).wait_recv()
-            total = total + landed[ll, j].astype(f32)
+        g = layer * per_owner + j
+        total = terms[g].astype(f32)
+        for step in range(1, half_l + 1):
+            slot = half_l if step == half_l else lax.rem(place + step, half_l)
+            owner_copy(g, slot).wait_recv()
+            total = total + landed[slot, j].astype(f32)
         scores[j * rows : (j + 1) * rows, :] = total
 
     for copy in sent:
         copy.wait_send()
-    for owner, copy in term_copies:
-
-        @pl.when(owner != layer)
+    for g in term_sent:
+
+        @pl.when(g // per_owner != layer)
         def _():
-            copy.wait_send()
+            owner_copy(g, 0).wait_send()
 
 
 def solution(mesh):
@@ -278,7 +308,7 @@
         proj = inward.shape[0]
         total = n_blk * n_shard
         per_owner = total // n_layer
-        tiles = 4
+        tiles = 2
         relay = 2 * (n_y - 1) * (n_shard - 1)
         sends = 2 * (n_y - 1 + n_shard - 1) + relay + 2 * n_y * n_shard * (n_core - 1)
         dma = pltpu.SemaphoreType.DMA
@@ -296,14 +326,16 @@
                 pltpu.VMEM((rows * proj // 2, 2 * proj), f32),
                 pltpu.VMEM((total, 2, rows // 2, grad), bf16),
                 pltpu.VMEM((total, rows, count), bf16),
-                pltpu.VMEM((n_layer, per_owner, rows, count), bf16),
+                pltpu.VMEM((n_layer // 2 + 1, per_owner, rows, count), bf16),
+                pltpu.VMEM((n_layer // 2, total, rows, count), bf16),
                 dma((tiles,)),
                 dma((3,)),
                 dma((sends,)),
                 dma((n_y, n_shard, 2)),
                 dma((n_y, n_shard, 2)),
                 dma((total,)),
-                dma((n_layer, per_owner)),
+                dma((n_layer // 2 + 1, per_owner)),
+                dma((n_layer // 2, total)),
             ],
             compiler_params=pltpu.CompilerParams(
                 collective_id=0, has_side_effects=True, vmem_limit_bytes=56 * 1024 * 1024

time: 35.8 us -> 32.2 us (0.90)
  Pallas kernels: 34 us -> 30.4 us
    pallas_call x1, Pallas kernels: 34 us -> 30.4 us  [per_device(): pl.pallas_call(functools.partial(kernel, (n_blk, n_layer, n_shard)), out_...]
where the time goes in v2:
time: 32.2 us; the launch traced here: 32.1 us
  Pallas kernels  30.4 us (94%)
  local copies, waits for them, and re-layouts  1.67 us (5%)
    pallas_call x1, Pallas kernels, per_device(): pl.pallas_call(functools.partial(kernel, (n_blk, n_layer, n_shard)), out_...  30.4 us
    unnamed x1, local copies, waits for them, and re-layouts  1.67 us

profile of v2, /device:TPU:4, one launch (start us, length us, event | category | flops | bytes accessed | tf_op | source)
XLA Modules:
  0.0 32.1 jit_solution(14192999421813188691)
XLA Ops:
  0.0 30.4 %shard_map.46 = f32[64,1024]{1,0:T(8,128)} custom-call(bf16[1024,4096]{1,0:T(8,128)(2,1)} %bitcast.4, bf16[32,4096]{1,0:T(8,128)(2,1)} %bitcast.5, bf16[64,64]{1,0:T(8,128)(2,1)} %bitcast.6, bf16[64,64]{1,0:T(8,128)(2,1)} %bitcast.7), custom_call_target="tpu_custom_call" | custom-call | tf_op jit(solution)/shard_map/pallas_call | solution.py:315
  30.4 1.7 %copy.6 = f32[64,1024]{1,0:T(8,128)} copy(f32[64,1024]{1,0:T(8,128)} %shard_map.46) | data formatting | bytes 524288
